TPU v7x, 256 devices: a whole 4x4x8 slice. The times are simulated.
256 devices in a mesh: gx: 8 (over z_lo, y), gy: 4 (over x), gz: 8 (over z_hi, core).
Axes of the slice: x: 4, y: 4, z: 8 (z_hi: 4, z_lo: 2; z = z_hi * 2 + z_lo), core: 2. Of those that a mesh axis runs over, the one named last changes fastest.
Arguments:
- coordinates: float32 [8, 4, 8, 3, 16, 128], P('gx', 'gy', 'gz'), may hold values from -8 to 168
- neighbours: int32 [8, 4, 8, 16, 128], P('gx', 'gy', 'gz'), may hold values from 0 to 991, as said below
- pair_index: int32 [8, 4, 8, 4, 15360], P('gx', 'gy', 'gz'), may hold values from 0 to 127, as said below
- pair_live: int32 [8, 4, 8, 15360], P('gx', 'gy', 'gz'), may hold values 0 or 1
- basis: bfloat16 [8, 4, 8, 128, 1536], P('gx', 'gy', 'gz'), may hold values from -50 to 50
Outputs:
- next_basis: float32 [8, 4, 8, 128, 1536], P('gx', 'gy', 'gz')
- ritz_matrix: float32 [256, 256], replicated
Inputs may be any that keep to these rules, and one draw needn't show every extreme that they name: neighbours[x, y, z, 0, f] = 864 + f. Any other entry c < 864 names frame c % 32 of the domain offset by (c // 32 // 9 - 1, c // 32 // 3 % 3 - 1, c // 32 % 3 - 1), which lies in the grid and is not the domain itself; an entry c >= 864 names the domain's own frame c - 864, never the row's frame f. `pair_index`: row 0 holds a frame f < 128, row 1 a slot 1 to 15, rows 2 and 3 atoms below 16.
All inputs are finite; a program needn't handle non-finite values. No bound on the sum of `pair_live` on one device may be relied on, other than what follows from the above.
Results may differ from a plain program's by a relative error of at most 0.0003.
Values may be sent and summed in bfloat16 or wider, within the bound.
A program may use at most 128 MiB of HBM per device.

v0:
```python
import jax
import jax.numpy as jnp
from jax import lax
from jax.sharding import Mesh
from jax.sharding import PartitionSpec as P

GX = ("gx_0", "gx_1")
GZ = ("gz_0", "gz_1")
stiffness = 0.01


def padded(cells, sides, width, closed):
    for axis, dim in sides:
        count = lax.axis_size(axis)
        ends = count if closed else count - 1
        head = lax.slice_in_dim(cells, 0, width, axis=dim)
        tail = lax.slice_in_dim(cells, cells.shape[dim] - width, cells.shape[dim], axis=dim)
        cells = jnp.concatenate(
            [
                lax.ppermute(tail, axis, [(i, (i + 1) % count) for i in range(ends)]),
                cells,
                lax.ppermute(head, axis, [((i + 1) % count, i) for i in range(ends)]),
            ],
            axis=dim,
        )
    return cells


def rows_for(lines, size):
    spare = -len(lines) % size
    return jnp.pad(lines, [(0, spare)] + [(0, 0)] * (lines.ndim - 1))


def sum_in_two_steps(x, near, far):
    lines = x.reshape(-1, *x.shape[1:][-1:])
    padded = rows_for(lines, lax.axis_size(near))
    own = lax.psum_scatter(padded, near, scatter_dimension=0, tiled=True)
    own = lax.psum(own, far)
    whole = lax.all_gather(own, near, axis=0, tiled=True)
    return whole[: len(lines)].reshape(x.shape)


def cross_product(left, right):
    return jnp.stack(
        [
            left[1] * right[2] - left[2] * right[1],
            left[2] * right[0] - left[0] * right[2],
            left[0] * right[1] - left[1] * right[0],
        ]
    )


def assemble(visible, neighbours, pair_index, pair_live):
    columns = visible.shape[2]
    frames = neighbours.shape[1]
    slots = neighbours.shape[0]
    centres = jnp.mean(visible, axis=1)
    own_frame = pair_index[0]
    slot_of = pair_index[1]
    atom_a = pair_index[2]
    atom_b = pair_index[3]
    self_column = own_frame + (columns - frames)
    partner = jnp.take(neighbours.reshape(-1), slot_of * frames + own_frame, axis=0)
    flat_coords = visible.reshape(3, -1)
    pos_a = jnp.take(flat_coords, atom_a * columns + self_column, axis=1)
    pos_b = jnp.take(flat_coords, atom_b * columns + partner, axis=1)
    arm_a = pos_a - jnp.take(centres, self_column, axis=1)
    arm_b = pos_b - jnp.take(centres, partner, axis=1)
    spring = pos_a - pos_b
    length_sq = jnp.maximum(jnp.sum(spring * spring, axis=0), 1.0)
    weight = stiffness * pair_live.astype(jnp.float32) / length_sq
    left_vec = jnp.concatenate([spring, cross_product(arm_a, spring)], axis=0)
    right_vec = jnp.concatenate([spring, cross_product(arm_b, spring)], axis=0)
    off_terms = -(weight * left_vec)[:, None, :] * right_vec[None, :, :]
    self_terms = (weight * left_vec)[:, None, :] * left_vec[None, :, :]
    values = jnp.concatenate([off_terms.reshape(36, -1).T, self_terms.reshape(36, -1).T], axis=0)
    row_keys = jnp.concatenate([slot_of * frames + own_frame, own_frame], axis=0)
    blocks = jnp.zeros((slots * frames, 36), jnp.float32).at[row_keys].add(values)
    return blocks.reshape(slots, frames, 36)


def apply_blocks(blocks, neighbours, vector_table):
    frames = neighbours.shape[1]
    vector_count = vector_table.shape[1] // 6

    def add_slot(slot_index, totals):
        gathered = jnp.take(vector_table, neighbours[slot_index], axis=0)
        coeffs = blocks[slot_index]
        pieces = [
            gathered[:, inner_dof * vector_count : (inner_dof + 1) * vector_count]
            for inner_dof in range(6)
        ]
        updated = []
        for outer_dof in range(6):
            total = totals[outer_dof]
            for inner_dof in range(6):
                column = coeffs[:, 6 * outer_dof + inner_dof : 6 * outer_dof + inner_dof + 1]
                total = total + column * pieces[inner_dof].astype(jnp.float32)
            updated.append(total)
        return tuple(updated)

    start = tuple((jnp.zeros((frames, vector_count), jnp.float32) for outer_dof in range(6)))
    totals = lax.fori_loop(0, neighbours.shape[0], add_slot, start)
    return jnp.concatenate(totals, axis=1)


def gram_matrix(left, right):
    return lax.dot_general(
        left, right, (((0,), (0,)), ((), ())), preferred_element_type=jnp.float32
    )


def rayleigh_ritz(basis_gram, cross_gram, image_gram, image_rows, total_rows):
    factor = jnp.linalg.cholesky(basis_gram / total_rows)
    sym_cross = (cross_gram + cross_gram.T) / (2.0 * total_rows)
    half_solved = lax.linalg.triangular_solve(factor, sym_cross, left_side=True, lower=True)
    ritz_matrix = lax.linalg.triangular_solve(factor, half_solved.T, left_side=True, lower=True)
    image_factor = jnp.linalg.cholesky(image_gram / total_rows)
    next_rows = lax.linalg.triangular_solve(
        image_factor, image_rows, left_side=False, lower=True, transpose_a=True
    )
    return (ritz_matrix, next_rows)


def per_device(coordinates, neighbours, pair_index, pair_live, basis):
    frames = basis.shape[3]
    vector_count = basis.shape[4] // 6
    rim_frames = frames // 4
    atoms_per = coordinates.shape[4]
    total_rows = 6 * frames * lax.axis_size(GX) * lax.axis_size("gy") * lax.axis_size(GZ)
    own_basis = basis[0, 0, 0]
    own_lists = neighbours[0, 0, 0]
    flat_basis = own_basis.reshape(frames * 6, vector_count)
    basis_local = gram_matrix(flat_basis, flat_basis)
    near_coords = padded(
        coordinates[:, :, :, :, :, :rim_frames], ((GX, 0), ("gy", 1), (GZ, 2)), 1, False
    )
    rim_rows = basis[:, :, :, :rim_frames, :]
    near_basis = padded(rim_rows, ((GX, 0), ("gy", 1), (GZ, 2)), 1, False)
    ghost_coords = (
        near_coords.reshape(27, 3, atoms_per, rim_frames)
        .transpose(1, 2, 0, 3)
        .reshape(3, atoms_per, 27 * rim_frames)
    )
    visible = jnp.concatenate([ghost_coords, coordinates[0, 0, 0]], axis=2)
    blocks = assemble(visible, own_lists, pair_index[0, 0, 0], pair_live[0, 0, 0])
    vector_table = jnp.concatenate(
        [near_basis.reshape(27 * rim_frames, 6 * vector_count), own_basis], axis=0
    )
    image_rows = apply_blocks(blocks, own_lists, vector_table)
    rounded = image_rows.astype(jnp.bfloat16).reshape(frames * 6, vector_count)
    cross_local = gram_matrix(flat_basis, rounded)
    image_local = gram_matrix(rounded, rounded)
    basis_gram, cross_gram, image_gram = (
        sum_in_two_steps(basis_local, "gz_1", ("gx_0", "gx_1", "gy", "gz_0")),
        sum_in_two_steps(cross_local, "gz_1", ("gx_0", "gx_1", "gy", "gz_0")),
        sum_in_two_steps(image_local, "gz_1", ("gx_0", "gx_1", "gy", "gz_0")),
    )
    ritz_matrix, next_rows = rayleigh_ritz(
        basis_gram, cross_gram, image_gram, image_rows.reshape(frames * 6, vector_count), total_rows
    )
    next_basis = next_rows.reshape(1, 1, 1, frames, 6 * vector_count)
    return (next_basis, ritz_matrix)


def solution(mesh):
    torus = Mesh(
        mesh.devices.reshape(2, 4, mesh.shape["gy"], 4, 2), ("gx_0", "gx_1", "gy", "gz_0", "gz_1")
    )
    in_specs = (
        P(GX, "gy", GZ, None, None, None),
        P(GX, "gy", GZ, None, None),
        P(GX, "gy", GZ, None, None),
        P(GX, "gy", GZ, None),
        P(GX, "gy", GZ, None, None),
    )
    out_specs = (P(GX, "gy", GZ, None, None), P())
    return jax.shard_map(
        per_device, mesh=torus, in_specs=in_specs, out_specs=out_specs, check_vma=False
    )
```

profile of v0, /device:TPU:1, one launch (start us, length us, event | category | flops | bytes accessed | tf_op | source)
XLA Modules:
  0.0 1204.4 jit_solution(14516050575677457552)
XLA Ops:
  7.2 4.0 collective-permute-start
  13.5 4.0 collective-permute-start.6
  24.2 84.9 %gather_fusion.1 = s32[15360]{0:T(1024)S(1)} fusion(s32[2048]{0:T(1024)S(1)} %bitcast.221, s32[15360]{0:T(1024)S(1)} %broadcast_clamp_fusion), kind=kCustom, calls=%fused_computation.5 | custom fusion | bytes 184320 | tf_op jit(solution)/shard_map/jit(_take)/gather | solution.py:63
  118.4 7.7 collective-permute-start.4
  129.0 5.3 collective-permute-done.5
  134.9 4.6 copy.145
  139.6 54.4 %gather_fusion.3 = f32[15360,3]{1,0:T(8,128)} fusion(f32[3,15872]{0,1:T(8,128)} %bitcast.223, s32[15360]{0:T(1024)S(1)} %get-tuple-element.414), kind=kCustom, calls=%fused_computation.3.clone | custom fusion | bytes 430080 | tf_op jit(solution)/shard_map/jit(_take)/gather | solution.py:66
  194.0 5.0 copy.147
  199.3 51.1 %gather_fusion.5 = f32[15360,3]{1,0:T(8,128)} fusion(f32[3,992]{0,1:T(8,128)S(1)} %broadcast_multiply_fusion.2, s32[15360]{0:T(1024)S(1)} %get-tuple-element.413), kind=kCustom, calls=%fused_computation.4.clone | custom fusion | bytes 430080 | tf_op jit(solution)/shard_map/jit(_take)/gather | solution.py:68
  250.4 5.0 copy.150
  255.4 54.4 %gather_fusion.2 = f32[15360,3]{1,0:T(8,128)} fusion(f32[3,15872]{0,1:T(8,128)} %bitcast.224, s32[15360]{0:T(1024)S(1)} %get-tuple-element.418), kind=kCustom, calls=%fused_computation.clone | custom fusion | bytes 430080 | tf_op jit(solution)/shard_map/jit(_take)/gather | solution.py:65
  309.9 5.0 copy.146
  314.9 51.1 %gather_fusion.4 = f32[15360,3]{1,0:T(8,128)} fusion(f32[3,992]{0,1:T(8,128)S(1)} %broadcast_multiply_fusion.2, s32[15360]{0:T(1024)S(1)} %get-tuple-element.417), kind=kCustom, calls=%fused_computation.1.clone | custom fusion | bytes 430080 | tf_op jit(solution)/shard_map/jit(_take)/gather | solution.py:67
  366.1 5.0 copy.149
  392.9 4.2 pad_maximum_fusion
  397.1 10.4 copy.151
  407.5 163.6 %scatter_custom_fusion = f32[2048,36]{1,0:T(8,128)S(1)} fusion(s32[30720]{0:T(1024)} %bitcast.248, f32[30720,36]{1,0:T(8,128)} %copy.151, f32[]{:T(128)} %constant.163.clone.1), kind=kCustom, calls=%fused_computation.145 | custom fusion | flops 1105920 | bytes 295424 | tf_op jit(solution)/shard_map/scatter-add | solution.py:78
  574.2 217.5 %while.30 = (s32[]{:T(128)}, f32[128,256]{1,0:T(8,128)}, f32[128,256]{1,0:T(8,128)}, f32[128,256]{1,0:T(8,128)}, f32[128,256]{1,0:T(8,128)}, /*index=5*/f32[128,...) while((s32[]{:T(128)}, f32[128,256]{1,0:T(8,128)}, ...), condition=%wide.region_4.7_spmd.clone, body=%wide.region_3.6_spmd.clone.sunk | while | flops 3934339 | bytes 5604240 | solution.py:103
  799.9 21.3 %reduce-scatter.8.cloned.1.call-done = f32[128,256]{0,1:T(8,128)} async-done(((f32[256,256]{0,1:T(8,128)}), f32[128,256]{0,1:T(8,128)}) %reduce-scatter.8.cloned.1.call-update) | async-done | bytes 131088 | tf_op jit(solution)/shard_map/reduce_scatter | solution.py:37
  821.2 17.4 %reduce-scatter.4.cloned.1.call-done = f32[128,256]{0,1:T(8,128)} async-done(((f32[256,256]{0,1:T(8,128)}), f32[128,256]{0,1:T(8,128)}) %reduce-scatter.4.cloned.1.call-update) | async-done | bytes 131088 | tf_op jit(solution)/shard_map/reduce_scatter | solution.py:37
  838.8 219.5 %all-reduce.4.cloned.1.call-done = (f32[128,256]{0,1:T(8,128)}, f32[128,256]{0,1:T(8,128)}, f32[128,256]{0,1:T(8,128)}) async-done(((f32[128,256]{0,1:T(8,128)}, f32[128,256]{0,1:T(8,128)}, f32[128,256]{0,1:T(8,128)}), (f32[128,256]{0,1:T(8,128)}, f32[128,256]{0,1:T(8,128)}, f32[128,256]{0,1:T(8,128)})) %all-reduce.4.cloned.1.call-update) | async-done | bytes 393232 | tf_op jit(solution)/shard_map/psum | solution.py:38
  1058.3 7.3 all_gather.10
  1065.9 11.7 cholesky.164
  1077.7 9.8 custom-call.24
  1088.0 11.7 cholesky.181
  1102.5 4.3 while.31
  1106.9 19.7 %custom-call.26 = f32[2,128,128]{1,2,0:T(8,128)S(1)} custom-call(f32[2,128,128]{2,1,0:T(8,128)S(1)} %get-tuple-element.242), custom_call_target="InvertDiagBlocksLowerTriangular" | custom-call | tf_op jit(solution)/shard_map/triangular_solve/custom-call.4 | solution.py:117
  1133.8 11.7 cholesky.130
  1145.5 9.8 custom-call.23
  1155.8 11.7 cholesky.147
  1170.3 4.2 while.29
  1174.5 19.7 %custom-call.14 = f32[2,128,128]{1,2,0:T(8,128)S(1)} custom-call(f32[2,128,128]{2,1,0:T(8,128)S(1)} %get-tuple-element.201), custom_call_target="InvertDiagBlocksLowerTriangular" | custom-call | tf_op jit(solution)/shard_map/triangular_solve | solution.py:119
  (386 shorter events, 294.4 us)
Async XLA Ops:
  7.2 17.0 %copy-start.11 = (s32[1,1,1,15360]{3,2,1,0:T(1,128)S(1)}, s32[1,1,1,15360]{3,2,1,0:T(1,128)}, u32[]{:S(2)}) copy-start(s32[1,1,1,15360]{3,2,1,0:T(1,128)} %param.17) | copy-start | bytes 184324
  7.2 17.0 %copy-start = (s32[1,1,1,16,128]{4,3,2,1,0:T(8,128)S(1)}, s32[1,1,1,16,128]{4,3,2,1,0:T(8,128)}, u32[]{:S(2)}) copy-start(s32[1,1,1,16,128]{4,3,2,1,0:T(8,128)} %param.15) | copy-start | bytes 24580
  7.2 792.7 %reduce-scatter.6.cloned.1.call-start = ((), (), s32[]{:S(2)}) async-start(), calls=%async_computation.4 | async-start | bytes 393216 | tf_op jit(solution)/shard_map/reduce_scatter | solution.py:37
  7.2 102.8 %collective-permute-start = (f32[1,1,1,3,16,32]{5,4,3,2,1,0:T(8,128)}, f32[1,1,1,3,16,32]{5,4,3,2,1,0:T(8,128)S(1)}, u32[]{:S(2)}, u32[]{:S(2)}) collective-permute-start(f32[1,1,1,3,16,32]{5,4,3,2,1,0:T(8,128)} %bitcast.240), channel_id=1, source_target_pairs={{0,32},{32,64},{64,96},{96,128},{128,160},{160,192},{192,224},{1,3... | collective-permute-start | bytes 18440 | tf_op jit(solution)/shard_map/ppermute | solution.py:20
  11.3 98.8 %collective-permute-start.1 = (f32[1,1,1,3,16,32]{5,4,3,2,1,0:T(8,128)}, f32[1,1,1,3,16,32]{5,4,3,2,1,0:T(8,128)S(1)}, u32[]{:S(2)}, u32[]{:S(2)}) collective-permute-start(f32[1,1,1,3,16,32]{5,4,3,2,1,0:T(8,128)} %bitcast.241), channel_id=1, source_target_pairs={{32,0},{64,32},{96,64},{128,96},{160,128},{192,160},{224,192},{33,... | collective-permute-start | bytes 18440 | tf_op jit(solution)/shard_map/ppermute | solution.py:22
  13.5 359.4 %collective-permute-start.6 = (bf16[1,1,1,32,1536]{4,3,2,1,0:T(8,128)(2,1)S(1)}, bf16[1,1,1,32,1536]{4,3,2,1,0:T(8,128)(2,1)S(1)}, u32[]{:S(2)}, u32[]{:S(2)}) collective-permute-start(bf16[1,1,1,32,1536]{4,3,2,1,0:T(8,128)(2,1)S(1)} %slice.420), channel_id=1, source_target_pairs={{0,32},{32,64},{64,96},{96,128},{128,160},{160,192},{192,224},{1,3... | collective-permute-start | bytes 294920 | tf_op jit(solution)/shard_map/ppermute | solution.py:20
  17.5 355.4 %collective-permute-start.7 = (bf16[1,1,1,32,1536]{4,3,2,1,0:T(8,128)(2,1)S(1)}, bf16[1,1,1,32,1536]{4,3,2,1,0:T(8,128)(2,1)S(1)}, u32[]{:S(2)}, u32[]{:S(2)}) collective-permute-start(bf16[1,1,1,32,1536]{4,3,2,1,0:T(8,128)(2,1)S(1)} %slice.420), channel_id=1, source_target_pairs={{32,0},{64,32},{96,64},{128,96},{160,128},{192,160},{224,192},{33,... | collective-permute-start | bytes 294920 | tf_op jit(solution)/shard_map/ppermute | solution.py:22
  20.1 89.1 %copy-start.2 = (bf16[768,256]{1,0:T(8,128)(2,1)}, bf16[768,256]{1,0:T(8,128)(2,1)S(1)}, u32[]{:S(2)}) copy-start(bf16[768,256]{1,0:T(8,128)(2,1)S(1)} %reshape_squeeze.7) | copy-start | bytes 1179652
  21.1 800.0 %reduce-scatter.8.cloned.1.call-start = ((), (), s32[]{:S(2)}) async-start(), calls=%async_computation.5 | async-start | bytes 393216 | tf_op jit(solution)/shard_map/reduce_scatter | solution.py:37
  24.2 85.9 %copy-start.8 = (f32[1,1,1,3,16,128]{5,4,3,2,1,0:T(8,128)S(1)}, f32[1,1,1,3,16,128]{5,4,3,2,1,0:T(8,128)}, u32[]{:S(2)}) copy-start(f32[1,1,1,3,16,128]{5,4,3,2,1,0:T(8,128)} %param.14) | copy-start | bytes 73732
  110.1 4.5 collective-permute-start.2
  113.2 5.1 collective-permute-start.3
  118.4 10.6 collective-permute-start.4
  126.1 8.2 collective-permute-start.5
  372.9 12.2 %copy-start.6 = (bf16[1,1,1,32,1536]{4,3,2,1,0:T(8,128)(2,1)}, bf16[1,1,1,32,1536]{4,3,2,1,0:T(8,128)(2,1)S(1)}, u32[]{:S(2)}) copy-start(bf16[1,1,1,32,1536]{4,3,2,1,0:T(8,128)(2,1)S(1)} %collective-permute-done.7) | copy-start | bytes 294916
  373.6 11.4 collective-permute-start.8
  376.8 8.3 collective-permute-start.9
  381.6 11.3 copy-start.1
  385.0 12.1 %copy-start.5 = (bf16[3,1,1,32,1536]{4,3,2,1,0:T(8,128)(2,1)}, bf16[3,1,1,32,1536]{4,3,2,1,0:T(8,128)(2,1)S(1)}, u32[]{:S(2)}) copy-start(bf16[3,1,1,32,1536]{4,3,2,1,0:T(8,128)(2,1)S(1)} %collective-permute-done.8) | copy-start | bytes 884740
  387.2 185.0 %collective-permute-start.10 = (bf16[3,3,1,32,1536]{4,3,2,1,0:T(8,128)(2,1)}, bf16[3,3,1,32,1536]{4,3,2,1,0:T(8,128)(2,1)}, u32[]{:S(2)}, u32[]{:S(2)}) collective-permute-start(bf16[3,3,1,32,1536]{4,3,2,1,0:T(8,128)(2,1)} %pad_maximum_fusion.3), channel_id=1, source_target_pairs={{0,1},{1,2},{2,3},{3,4},{4,5},{5,6},{6,7},{8,9},{9,10},{10,11},{11... | collective-permute-start | bytes 2654216 | tf_op jit(solution)/shard_map/ppermute | solution.py:20
  389.7 182.5 %collective-permute-start.11 = (bf16[3,3,1,32,1536]{4,3,2,1,0:T(8,128)(2,1)}, bf16[3,3,1,32,1536]{4,3,2,1,0:T(8,128)(2,1)}, u32[]{:S(2)}, u32[]{:S(2)}) collective-permute-start(bf16[3,3,1,32,1536]{4,3,2,1,0:T(8,128)(2,1)} %pad_maximum_fusion.3), channel_id=1, source_target_pairs={{1,0},{2,1},{3,2},{4,3},{5,4},{6,5},{7,6},{9,8},{10,9},{11,10},{12... | collective-permute-start | bytes 2654216 | tf_op jit(solution)/shard_map/ppermute | solution.py:22
  397.1 175.1 %copy-start.7 = (bf16[1,1,1,32,1536]{4,3,2,1,0:T(8,128)(2,1)S(1)}, bf16[1,1,1,32,1536]{4,3,2,1,0:T(8,128)(2,1)}, u32[]{:S(2)}) copy-start(bf16[1,1,1,32,1536]{4,3,2,1,0:T(8,128)(2,1)} %copy-done.6) | copy-start | bytes 294916
  571.1 2.9 copy-start.4
  791.7 6.0 copy-start.3
  798.8 39.8 %reduce-scatter.4.cloned.1.call-start = ((), (), s32[]{:S(2)}) async-start(), calls=%async_computation.3 | async-start | bytes 393216 | tf_op jit(solution)/shard_map/reduce_scatter | solution.py:37
  799.8 258.5 %all-reduce.4.cloned.1.call-start = ((), (), s32[]{:S(2)}) async-start(), calls=%async_computation.6 | async-start | bytes 786432 | tf_op jit(solution)/shard_map/psum | solution.py:38
  1058.3 68.2 %copy-start.10 = (f32[128,256]{0,1:T(8,128)S(1)}, f32[128,256]{0,1:T(8,128)}, u32[]{:S(2)}) copy-start(f32[128,256]{0,1:T(8,128)} %get-tuple-element.340) | copy-start | bytes 393220
  1102.4 29.1 %copy-start.9 = (f32[128,256]{0,1:T(8,128)S(1)}, f32[128,256]{0,1:T(8,128)}, u32[]{:S(2)}) copy-start(f32[128,256]{0,1:T(8,128)} %get-tuple-element.339) | copy-start | bytes 393220
Sparse Core Ops, SparseCore 0:
  21.3 19.8 reduce-scatter.5
  798.9 22.2 reduce-scatter.7
  824.2 14.3 reduce-scatter.3
  844.2 214.0 all-reduce.3
where the time goes:
time: 1220 us; the launch traced here: 1200 us
  other arithmetic  469 us (38%)
  local copies, waits for them, and re-layouts  395 us (32%)
  waiting for transfers between devices  268 us (22%)
  starting transfers between devices  35 us (3%)
  between operations  17.6 us (1%)
    psum x1, waiting for transfers between devices, sum_in_two_steps(): own = lax.psum(own, far)  220 us
    scatter-add x1, other arithmetic, assemble(): jnp.zeros((slots * frames, 36), jnp.float32).at[row_keys].add(values)  164 us
    add x96, other arithmetic, add_slot(): total = total + column * pieces[inner_dof].astype(jnp.float32)  161 us
    gather x1, local copies, waits for them, and re-layouts, assemble(): jnp.take(neighbours.reshape(-1), slot_of * frames + own_frame, axis=0)  84.9 us
    gather x2, local copies, waits for them, and re-layouts, assemble(): pos_a = jnp.take(flat_coords, atom_a * columns + self_column, axis=1)  59.5 us
    gather x2, local copies, waits for them, and re-layouts, assemble(): pos_b = jnp.take(flat_coords, atom_b * columns + partner, axis=1)  59.4 us
    gather x2, local copies, waits for them, and re-layouts, assemble(): arm_a = pos_a - jnp.take(centres, self_column, axis=1)  56.2 us
    gather x2, local copies, waits for them, and re-layouts, assemble(): arm_b = pos_b - jnp.take(centres, partner, axis=1)  56.2 us
  transfers between devices with their start and end apart: 16, of which 6 were waited for; matrix products, arithmetic and copies ran while one was open for 62% of the time, Pallas kernels for 0%

commit v1 on v0

--- a/solution.py
+++ b/solution.py
@@ -35,7 +35,7 @@
     lines = x.reshape(-1, *x.shape[1:][-1:])
     padded = rows_for(lines, lax.axis_size(near))
     own = lax.psum_scatter(padded, near, scatter_dimension=0, tiled=True)
-    own = lax.psum(own, far)
+    own = jnp.sum(lax.all_gather(own, far), axis=0)
     whole = lax.all_gather(own, near, axis=0, tiled=True)
     return whole[: len(lines)].reshape(x.shape)
 

time: 1220 us -> 3230 us (2.65)
  waiting for transfers between devices: 268 us -> 1980 us
  blocking collectives: 11.3 us -> 297 us
    all_gather x0 -> x3, waiting for transfers between devices: none -> 1940 us  [sum_in_two_steps(): own = jnp.sum(lax.all_gather(own, far), axis=0)]
    all_gather x3, blocking collectives: 11.3 us -> 297 us  [sum_in_two_steps(): whole = lax.all_gather(own, near, axis=0, tiled=True)]
    psum x1 -> x0, waiting for transfers between devices: 220 us -> none  [sum_in_two_steps(): own = lax.psum(own, far)]
  transfers between devices with their start and end apart: 16 -> 18, of which waited for: 6 -> 8; matrix products, arithmetic and copies ran while one was open for 62% -> 27% of each run, Pallas kernels for 0% -> 0%
where the time goes in v1:
time: 3230 us; the launch traced here: 3210 us
  waiting for transfers between devices  1980 us (61%)
  other arithmetic  475 us (15%)
  local copies, waits for them, and re-layouts  396 us (12%)
  blocking collectives  297 us (9%)
  starting transfers between devices  40.8 us (1%)
    all_gather x3, waiting for transfers between devices, sum_in_two_steps(): own = jnp.sum(lax.all_gather(own, far), axis=0)  1940 us
    all_gather x3, blocking collectives, sum_in_two_steps(): whole = lax.all_gather(own, near, axis=0, tiled=True)  297 us
    scatter-add x1, other arithmetic, assemble(): jnp.zeros((slots * frames, 36), jnp.float32).at[row_keys].add(values)  164 us
    add x96, other arithmetic, add_slot(): total = total + column * pieces[inner_dof].astype(jnp.float32)  161 us
    gather x1, local copies, waits for them, and re-layouts, assemble(): jnp.take(neighbours.reshape(-1), slot_of * frames + own_frame, axis=0)  84.9 us
  transfers between devices with their start and end apart: 18, of which 8 were waited for; matrix products, arithmetic and copies ran while one was open for 27% of the time, Pallas kernels for 0%

profile of v1, /device:TPU:1, one launch (start us, length us, event | category | flops | bytes accessed | tf_op | source)
XLA Modules:
  0.0 3213.3 jit_solution(8397292651530636338)
XLA Ops:
  26.4 84.9 %gather_fusion.1 = s32[15360]{0:T(1024)S(1)} fusion(s32[2048]{0:T(1024)S(1)} %bitcast.228, s32[15360]{0:T(1024)S(1)} %broadcast_clamp_fusion), kind=kCustom, calls=%fused_computation.5 | custom fusion | bytes 184320 | tf_op jit(solution)/shard_map/jit(_take)/gather | solution.py:63
  118.2 6.7 collective-permute-start.5
  136.2 54.4 %gather_fusion.3 = f32[15360,3]{1,0:T(8,128)} fusion(f32[3,15872]{0,1:T(8,128)} %bitcast.230, s32[15360]{0:T(1024)S(1)} %get-tuple-element.411), kind=kCustom, calls=%fused_computation.3.clone | custom fusion | bytes 430080 | tf_op jit(solution)/shard_map/jit(_take)/gather | solution.py:66
  190.6 5.0 copy.137
  195.6 54.4 %gather_fusion.2 = f32[15360,3]{1,0:T(8,128)} fusion(f32[3,15872]{0,1:T(8,128)} %bitcast.231, s32[15360]{0:T(1024)S(1)} %get-tuple-element.415), kind=kCustom, calls=%fused_computation.clone | custom fusion | bytes 430080 | tf_op jit(solution)/shard_map/jit(_take)/gather | solution.py:65
  255.4 51.1 %gather_fusion.5 = f32[15360,3]{1,0:T(8,128)} fusion(f32[3,992]{0,1:T(8,128)S(1)} %broadcast_multiply_fusion.2, s32[15360]{0:T(1024)S(1)} %get-tuple-element.410), kind=kCustom, calls=%fused_computation.4.clone | custom fusion | bytes 430080 | tf_op jit(solution)/shard_map/jit(_take)/gather | solution.py:68
  311.5 51.1 %gather_fusion.4 = f32[15360,3]{1,0:T(8,128)} fusion(f32[3,992]{0,1:T(8,128)S(1)} %broadcast_multiply_fusion.2, s32[15360]{0:T(1024)S(1)} %get-tuple-element.414), kind=kCustom, calls=%fused_computation.1.clone | custom fusion | bytes 430080 | tf_op jit(solution)/shard_map/jit(_take)/gather | solution.py:67
  371.4 5.3 collective-permute-start.8
  387.8 5.7 collective-permute-start.10
  397.8 10.3 copy.141
  408.1 163.6 %scatter_custom_fusion = f32[2048,36]{1,0:T(8,128)S(1)} fusion(s32[30720]{0:T(1024)} %bitcast.258, f32[30720,36]{1,0:T(8,128)} %copy.141, f32[]{:T(128)} %constant.163.clone.1), kind=kCustom, calls=%fused_computation.146 | custom fusion | flops 1105920 | bytes 295424 | tf_op jit(solution)/shard_map/scatter-add | solution.py:78
  574.9 190.0 %while.30 = (s32[]{:T(128)}, f32[128,256]{1,0:T(8,128)}, f32[128,256]{1,0:T(8,128)}, f32[128,256]{1,0:T(8,128)}, f32[128,256]{1,0:T(8,128)}, /*index=5*/f32[128,...) while((s32[]{:T(128)}, f32[128,256]{1,0:T(8,128)}, ...), condition=%wide.region_4.7_spmd.clone, body=%wide.region_3.6_spmd.clone.sunk | while | flops 3934339 | bytes 5604248 | solution.py:103
  773.6 17.2 reduce-scatter.4.cloned.1.call-done
  790.9 17.3 reduce-scatter.8.cloned.1.call-done
  808.5 613.7 %all-gather.9.cloned.1.call-done = f32[16384,256]{1,0:T(8,128)} async-done(((f32[128,256]{1,0:T(8,128)}), f32[16384,256]{1,0:T(8,128)}) %all-gather.9.cloned.1.call-update) | async-done | bytes 16777232 | tf_op jit(solution)/shard_map/all_gather | solution.py:38
  1422.2 6.8 reduce_sum.48
  1429.1 92.9 %all_gather.32 = f32[256,256]{0,1:T(8,128)S(1)} all-gather(f32[128,256]{0,1:T(8,128)S(1)} %copy.147), channel_id=1, replica_groups=mesh['gx_0'=2,'gx_1'=4,'gy'=4,'gz_0'=4,'gz_1'=2] {'gz_1'}, dimensions={0}, use_global_device_ids=true | all-gather | bytes 393216 | tf_op jit(solution)/shard_map/all_gather | solution.py:39
  1522.3 11.7 cholesky.164
  1534.1 9.8 custom-call.24
  1544.3 11.7 cholesky.181
  1562.0 19.7 custom-call.26
  1581.6 635.5 %all-gather.7.cloned.1.call-done = f32[16384,256]{1,0:T(8,128)} async-done(((f32[128,256]{1,0:T(8,128)}), f32[16384,256]{1,0:T(8,128)}) %all-gather.7.cloned.1.call-update) | async-done | bytes 16777232 | tf_op jit(solution)/shard_map/all_gather | solution.py:38
  2217.1 6.8 reduce_sum.47
  2224.0 87.6 %all_gather.29 = f32[256,256]{0,1:T(8,128)S(1)} all-gather(f32[128,256]{0,1:T(8,128)S(1)} %copy.144), channel_id=1, replica_groups=mesh['gx_0'=2,'gx_1'=4,'gy'=4,'gz_0'=4,'gz_1'=2] {'gz_1'}, dimensions={0}, use_global_device_ids=true | all-gather | bytes 393216 | tf_op jit(solution)/shard_map/all_gather | solution.py:39
  2311.8 11.7 cholesky.130
  2323.6 9.8 custom-call.23
  2333.9 11.7 cholesky.147
  2352.4 19.7 custom-call.14
  2375.4 689.5 %all-gather.11.cloned.1.call-done = f32[16384,256]{0,1:T(8,128)} async-done(((f32[128,256]{0,1:T(8,128)}), f32[16384,256]{0,1:T(8,128)}) %all-gather.11.cloned.1.call-update) | async-done | bytes 16777232 | tf_op jit(solution)/shard_map/all_gather | solution.py:38
  3064.9 14.1 copy.154
  3079.0 8.4 bitcast_reduce_fusion
  3087.4 116.0 %all_gather.35 = f32[256,256]{0,1:T(8,128)S(1)} all-gather(f32[128,256]{0,1:T(8,128)S(1)} %bitcast_reduce_fusion), channel_id=1, replica_groups=mesh['gx_0'=2,'gx_1'=4,'gy'=4,'gz_0'=4,'gz_1'=2] {'gz_1'}, dimensions={0}, use_global_device_ids=true | all-gather | bytes 393216 | tf_op jit(solution)/shard_map/all_gather | solution.py:39
  (391 shorter events, 298.3 us)
Async XLA Ops:
  7.2 19.3 copy-start
  7.2 765.9 %reduce-scatter.6.cloned.1.call-start = ((), (), s32[]{:S(2)}) async-start(), calls=%async_computation.4 | async-start | bytes 393216 | tf_op jit(solution)/shard_map/reduce_scatter | solution.py:37
  7.2 104.3 %collective-permute-start.1 = (f32[1,1,1,3,16,32]{5,4,3,2,1,0:T(8,128)}, f32[1,1,1,3,16,32]{5,4,3,2,1,0:T(8,128)S(1)}, u32[]{:S(2)}, u32[]{:S(2)}) collective-permute-start(f32[1,1,1,3,16,32]{5,4,3,2,1,0:T(8,128)} %bitcast.250), channel_id=1, source_target_pairs={{32,0},{64,32},{96,64},{128,96},{160,128},{192,160},{224,192},{33,... | collective-permute-start | bytes 18440 | tf_op jit(solution)/shard_map/ppermute | solution.py:22
  8.5 103.0 %collective-permute-start = (f32[1,1,1,3,16,32]{5,4,3,2,1,0:T(8,128)}, f32[1,1,1,3,16,32]{5,4,3,2,1,0:T(8,128)S(1)}, u32[]{:S(2)}, u32[]{:S(2)}) collective-permute-start(f32[1,1,1,3,16,32]{5,4,3,2,1,0:T(8,128)} %bitcast.251), channel_id=1, source_target_pairs={{0,32},{32,64},{64,96},{96,128},{128,160},{160,192},{192,224},{1,3... | collective-permute-start | bytes 18440 | tf_op jit(solution)/shard_map/ppermute | solution.py:20
  14.1 355.3 %collective-permute-start.7 = (bf16[1,1,1,32,1536]{4,3,2,1,0:T(8,128)(2,1)S(1)}, bf16[1,1,1,32,1536]{4,3,2,1,0:T(8,128)(2,1)S(1)}, u32[]{:S(2)}, u32[]{:S(2)}) collective-permute-start(bf16[1,1,1,32,1536]{4,3,2,1,0:T(8,128)(2,1)S(1)} %slice.420), channel_id=1, source_target_pairs={{32,0},{64,32},{96,64},{128,96},{160,128},{192,160},{224,192},{33,... | collective-permute-start | bytes 294920 | tf_op jit(solution)/shard_map/ppermute | solution.py:22
  15.4 354.0 %collective-permute-start.6 = (bf16[1,1,1,32,1536]{4,3,2,1,0:T(8,128)(2,1)S(1)}, bf16[1,1,1,32,1536]{4,3,2,1,0:T(8,128)(2,1)S(1)}, u32[]{:S(2)}, u32[]{:S(2)}) collective-permute-start(bf16[1,1,1,32,1536]{4,3,2,1,0:T(8,128)(2,1)S(1)} %slice.420), channel_id=1, source_target_pairs={{0,32},{32,64},{64,96},{96,128},{128,160},{160,192},{192,224},{1,3... | collective-permute-start | bytes 294920 | tf_op jit(solution)/shard_map/ppermute | solution.py:20
  20.7 90.6 %copy-start.2 = (bf16[768,256]{1,0:T(8,128)(2,1)}, bf16[768,256]{1,0:T(8,128)(2,1)S(1)}, u32[]{:S(2)}) copy-start(bf16[768,256]{1,0:T(8,128)(2,1)S(1)} %reshape_squeeze.7) | copy-start | bytes 1179652
  21.8 769.1 %reduce-scatter.4.cloned.1.call-start = ((), (), s32[]{:S(2)}) async-start(), calls=%async_computation.3 | async-start | bytes 393216 | tf_op jit(solution)/shard_map/reduce_scatter | solution.py:37
  26.4 85.1 %copy-start.8 = (f32[1,1,1,3,16,128]{5,4,3,2,1,0:T(8,128)S(1)}, f32[1,1,1,3,16,128]{5,4,3,2,1,0:T(8,128)}, u32[]{:S(2)}) copy-start(f32[1,1,1,3,16,128]{5,4,3,2,1,0:T(8,128)} %param.14) | copy-start | bytes 73732
  111.5 5.3 collective-permute-start.3
  112.8 5.4 collective-permute-start.2
  118.2 11.5 collective-permute-start.5
  124.9 6.0 collective-permute-start.4
  369.4 14.4 copy-start.6
  370.2 13.6 collective-permute-start.9
  371.4 12.3 collective-permute-start.8
  380.4 13.2 copy-start.1
  383.8 14.0 copy-start.5
  385.9 186.9 %collective-permute-start.11 = (bf16[3,3,1,32,1536]{4,3,2,1,0:T(8,128)(2,1)}, bf16[3,3,1,32,1536]{4,3,2,1,0:T(8,128)(2,1)}, u32[]{:S(2)}, u32[]{:S(2)}) collective-permute-start(bf16[3,3,1,32,1536]{4,3,2,1,0:T(8,128)(2,1)} %pad_maximum_fusion.3), channel_id=1, source_target_pairs={{1,0},{2,1},{3,2},{4,3},{5,4},{6,5},{7,6},{9,8},{10,9},{11,10},{12... | collective-permute-start | bytes 2654216 | tf_op jit(solution)/shard_map/ppermute | solution.py:22
  387.8 185.0 %collective-permute-start.10 = (bf16[3,3,1,32,1536]{4,3,2,1,0:T(8,128)(2,1)}, bf16[3,3,1,32,1536]{4,3,2,1,0:T(8,128)(2,1)}, u32[]{:S(2)}, u32[]{:S(2)}) collective-permute-start(bf16[3,3,1,32,1536]{4,3,2,1,0:T(8,128)(2,1)} %pad_maximum_fusion.3), channel_id=1, source_target_pairs={{0,1},{1,2},{2,3},{3,4},{4,5},{5,6},{6,7},{8,9},{9,10},{10,11},{11... | collective-permute-start | bytes 2654216 | tf_op jit(solution)/shard_map/ppermute | solution.py:20
  397.8 175.1 %copy-start.7 = (bf16[1,1,1,32,1536]{4,3,2,1,0:T(8,128)(2,1)S(1)}, bf16[1,1,1,32,1536]{4,3,2,1,0:T(8,128)(2,1)}, u32[]{:S(2)}) copy-start(bf16[1,1,1,32,1536]{4,3,2,1,0:T(8,128)(2,1)} %copy-done.6) | copy-start | bytes 294916
  408.1 166.6 %copy-start.4 = (bf16[1,1,1,128,1536]{4,3,2,1,0:T(8,128)(2,1)S(1)}, bf16[1,1,1,128,1536]{4,3,2,1,0:T(8,128)(2,1)}, u32[]{:S(2)}) copy-start(bf16[1,1,1,128,1536]{4,3,2,1,0:T(8,128)(2,1)} %param.18) | copy-start | bytes 1179652
  764.9 7.0 copy-start.3
  771.9 36.4 %reduce-scatter.8.cloned.1.call-start = ((), (), s32[]{:S(2)}) async-start(), calls=%async_computation.5 | async-start | bytes 393216 | tf_op jit(solution)/shard_map/reduce_scatter | solution.py:37
  773.0 649.2 %all-gather.9.cloned.1.call-start = ((), (), s32[]{:S(2)}) async-start(), calls=%async_computation.7 | async-start | bytes 16908288 | tf_op jit(solution)/shard_map/all_gather | solution.py:38
  773.6 1443.5 %all-gather.7.cloned.1.call-start = ((), (), s32[]{:S(2)}) async-start(), calls=%async_computation.6 | async-start | bytes 16908288 | tf_op jit(solution)/shard_map/all_gather | solution.py:38
  790.9 2274.0 %all-gather.11.cloned.1.call-start = ((), (), s32[]{:S(2)}) async-start(), calls=%async_computation.8 | async-start | bytes 16908288 | tf_op jit(solution)/shard_map/all_gather | solution.py:38
Sparse Core Ops, SparseCore 0:
  21.9 22.0 reduce-scatter.5
  772.0 18.7 reduce-scatter.3
  793.9 14.3 reduce-scatter.7
  809.9 612.2 all-gather.8
  1423.8 793.2 all-gather.6
  2218.7 846.1 all-gather.10
